TPU v7x, 256 devices: a whole 4x4x8 slice. The times are simulated.
256 devices in a mesh: span: 64 (over y_hi, x, z), rows: 4 (over y_lo, core).
Axes of the slice: x: 4, y: 4 (y_hi: 2, y_lo: 2; y = y_hi * 2 + y_lo), z: 8, core: 2. Of those that a mesh axis runs over, the one named last changes fastest.
Arguments:
- pressure_source: float32 [256, 128, 1024], P('span', 'rows'), may hold values from -6 to 6
- geometry: float32 [64, 3, 128, 1024], P('span', None, 'rows'), may hold values from 0.1 to 1
- owner: int32 [1], replicated, may hold values from 0 to 63
Outputs:
- pressure: float32 [256, 128, 1024], P('span', 'rows')
Inputs may be any that keep to these rules, and one draw needn't show every extreme that they name: owner is a span index.
All inputs are finite; a program needn't handle non-finite values.
Results may differ from a plain program's by a relative error of at most 0.00011.
Values sent between devices are 32-bit elements; how exact they have to be, the bound alone decides.
A program may use at most 64 MiB of HBM per device.

v0:
```python
import math

import jax
import jax.numpy as jnp
from jax import lax
from jax.sharding import Mesh
from jax.sharding import PartitionSpec as P

SWEEPS = 2
STEPS = 8
SPAN = ("span_0", "span_1", "span_2")
ROWS = ("rows_0", "rows_1")


LOWER_BOUND = 0.02
UPPER_BOUND = 2.0
HIGHEST = lax.Precision.HIGHEST


def spread(x, axes, root):
    x = jnp.where(lax.axis_index(axes) == root, x, jnp.zeros_like(x))
    for axis in axes:
        x = lax.psum(x, axis)
    return x


def in_one_piece(arrays, axis, split_dim, concat_dim, along):
    ends, at = ([], 0)
    for a in arrays[:-1]:
        at += a.shape[along]
        ends.append(at)
    both = jnp.concatenate(arrays, axis=along)
    return tuple(
        jnp.split(
            lax.all_to_all(both, axis, split_axis=split_dim, concat_axis=concat_dim, tiled=True),
            ends,
            axis=along,
        )
    )


def in_blocks(x, dim, size):
    before, after = (x.shape[:dim], x.shape[dim + 1 :])
    return jnp.moveaxis(x.reshape(*before, size, -1, *after), dim, 0)


def laid_out(parts, dim):
    dims = list(parts.shape[1:])
    dims[dim] *= parts.shape[0]
    return jnp.moveaxis(parts, 0, dim).reshape(dims)


def moved_by_axis(parts, axes, order):
    dims = [lax.axis_size(a) for a in axes]
    parts = parts.reshape(*dims, *parts.shape[1:])
    for k in order:
        parts = lax.all_to_all(parts, axes[k], split_axis=k, concat_axis=k, tiled=True)
    return parts.reshape(-1, *parts.shape[len(axes) :])


def core_and_chips(x, groups, order, split_dim, concat_dim):
    size = lax.axis_size(groups[0]) * lax.axis_size(groups[1])
    parts = in_blocks(x, split_dim, size)
    return laid_out(moved_by_axis(parts, groups, order), concat_dim)


def side_by_side(arrays, axis, dim, along):
    ends, at = ([], 0)
    for a in arrays[:-1]:
        at += a.shape[along]
        ends.append(at)
    both = jnp.concatenate(arrays, axis=along)
    return tuple(jnp.split(lax.all_gather(both, axis, axis=dim, tiled=True), ends, axis=along))


def reverse_bits(number, bit_count):
    result = number * 0
    for level in range(bit_count):
        result = result + number // 2**level % 2 * 2 ** (bit_count - 1 - level)
    return result


def apply_faces(planes, upper_rows, lower_rows, coeffs):
    left_face, right_face, top_face, bottom_face, diagonal = coeffs
    zero_col = jnp.zeros_like(planes[:, :, :1])
    left_cols = jnp.concatenate([zero_col, planes[:, :, :-1]], axis=2)
    right_cols = jnp.concatenate([planes[:, :, 1:], zero_col], axis=2)
    return (
        diagonal * planes
        - left_face * left_cols
        - right_face * right_cols
        - top_face * upper_rows
        - bottom_face * lower_rows
    )


def plain_operator(planes, coeffs):
    zero_row = jnp.zeros_like(planes[:, :1])
    upper_rows = jnp.concatenate([zero_row, planes[:, :-1]], axis=1)
    lower_rows = jnp.concatenate([planes[:, 1:], zero_row], axis=1)
    return apply_faces(planes, upper_rows, lower_rows, coeffs)


def chebyshev(rhs, coeffs, operator):
    center = (UPPER_BOUND + LOWER_BOUND) / 2.0
    half_width = (UPPER_BOUND - LOWER_BOUND) / 2.0
    sigma_ratio = center / half_width
    inverse_diag = 1.0 / coeffs[4]
    solution = jnp.zeros_like(rhs)
    residual = rhs
    for sweep_index in range(SWEEPS):
        ratio_now = 1.0 / sigma_ratio
        direction = residual * inverse_diag / center
        for step_index in range(STEPS):
            solution = solution + direction
            residual = residual - operator(direction, coeffs)
            ratio_next = 1.0 / (2.0 * sigma_ratio - ratio_now)
            direction = (
                ratio_next * ratio_now * direction
                + 2.0 * ratio_next / half_width * residual * inverse_diag
            )
            ratio_now = ratio_next
    return solution


def on_device(pressure_source, geometry, owner):
    span_count = lax.axis_size(SPAN)
    device = lax.axis_index(SPAN)
    bit_count = span_count.bit_length() - 1
    local_count, row_count, col_count = pressure_source.shape
    total_len = local_count * span_count
    plane = spread(geometry[0], SPAN, owner[0])
    west_face = plane[0]
    north_face = plane[1]
    volume = plane[2]
    merged = pressure_source.reshape((1, local_count * row_count, col_count))
    received = lax.all_to_all(merged, SPAN, split_axis=1, concat_axis=0, tiled=True)
    positions = jnp.arange(span_count, dtype=jnp.int32)
    freqs = reverse_bits(positions, bit_count)
    phase = (freqs[:, None] * positions[None, :] % span_count).astype(jnp.float32) * (
        -2.0 * math.pi / span_count
    )
    real_rows = jnp.einsum("rd,dtc->rtc", jnp.cos(phase), received, precision=HIGHEST)
    imag_rows = jnp.einsum("rd,dtc->rtc", jnp.sin(phase), received, precision=HIGHEST)
    real_back, imag_back = in_one_piece((real_rows, imag_rows), SPAN, 0, 1, 2)
    real_part = real_back.reshape(pressure_source.shape)
    imag_part = imag_back.reshape(pressure_source.shape)
    frequency = reverse_bits(device, bit_count)
    local_index = jnp.arange(local_count, dtype=jnp.int32)
    mode_index = frequency + span_count * local_index
    forward_phase = (mode_index[:, None] * local_index[None, :] % total_len).astype(jnp.float32) * (
        -2.0 * math.pi / total_len
    )
    forward_cos = jnp.cos(forward_phase)
    forward_sin = jnp.sin(forward_phase)
    spec_real = jnp.einsum("kj,jyc->kyc", forward_cos, real_part, precision=HIGHEST) - jnp.einsum(
        "kj,jyc->kyc", forward_sin, imag_part, precision=HIGHEST
    )
    spec_imag = jnp.einsum("kj,jyc->kyc", forward_sin, real_part, precision=HIGHEST) + jnp.einsum(
        "kj,jyc->kyc", forward_cos, imag_part, precision=HIGHEST
    )
    eigen = 2.0 - 2.0 * jnp.cos(mode_index.astype(jnp.float32) * (2.0 * math.pi / total_len))
    eigen_both = jnp.concatenate([eigen, eigen], axis=0)
    stacked = jnp.concatenate([spec_real, spec_imag], axis=0)
    rows_count = lax.axis_size(ROWS)
    row_device = lax.axis_index(ROWS)
    per_device = 2 * local_count // rows_count
    mine = core_and_chips(stacked, ("rows_0", "rows_1"), (1, 0), 0, 1)
    west_all, north_all, volume_all = side_by_side((west_face, north_face, volume), ROWS, 0, 1)
    east_all = jnp.concatenate([west_all[:, 1:], jnp.zeros_like(west_all[:, :1])], axis=1)
    south_all = jnp.concatenate([north_all[1:], jnp.zeros_like(north_all[:1])], axis=0)
    face_total = west_all + east_all + north_all + south_all
    eigen_mine = lax.dynamic_slice_in_dim(eigen_both, row_device * per_device, per_device)
    diagonal = face_total[None] + eigen_mine[:, None, None] * volume_all[None]
    coeffs = (west_all, east_all, north_all, south_all, diagonal)
    solved_mine = chebyshev(mine, coeffs, plain_operator)
    solved = lax.all_to_all(solved_mine, ROWS, split_axis=1, concat_axis=0, tiled=True)
    solved_real = solved[:local_count]
    solved_imag = solved[local_count:]
    inverse_cos = jnp.transpose(forward_cos) / local_count
    inverse_sin = -jnp.transpose(forward_sin) / local_count
    real_part = jnp.einsum("jk,kyc->jyc", inverse_cos, solved_real, precision=HIGHEST) - jnp.einsum(
        "jk,kyc->jyc", inverse_sin, solved_imag, precision=HIGHEST
    )
    imag_part = jnp.einsum("jk,kyc->jyc", inverse_sin, solved_real, precision=HIGHEST) + jnp.einsum(
        "jk,kyc->jyc", inverse_cos, solved_imag, precision=HIGHEST
    )
    merged_real = real_part.reshape((1, local_count * row_count, col_count))
    merged_imag = imag_part.reshape((1, local_count * row_count, col_count))
    recv_real, recv_imag = in_one_piece((merged_real, merged_imag), SPAN, 1, 0, 2)
    positions = jnp.arange(span_count, dtype=jnp.int32)
    freqs = reverse_bits(positions, bit_count)
    phase = (positions[:, None] * freqs[None, :] % span_count).astype(jnp.float32) * (
        2.0 * math.pi / span_count
    )
    gathered_rows = (
        jnp.einsum("ds,stc->dtc", jnp.cos(phase), recv_real, precision=HIGHEST)
        - jnp.einsum("ds,stc->dtc", jnp.sin(phase), recv_imag, precision=HIGHEST)
    ) / span_count
    pressure_back = lax.all_to_all(gathered_rows, SPAN, split_axis=0, concat_axis=1, tiled=True)
    return pressure_back.reshape(pressure_source.shape)


def solution(mesh):
    torus = Mesh(
        mesh.devices.reshape(2, 4, 8, 2, 2), ("span_0", "span_1", "span_2", "rows_0", "rows_1")
    )
    in_specs = (P(SPAN, ROWS, None), P(SPAN, None, ROWS, None), P())
    out_specs = P(SPAN, ROWS, None)
    return jax.shard_map(
        on_device, mesh=torus, in_specs=in_specs, out_specs=out_specs, check_vma=False
    )
```

profile of v0, /device:TPU:6, one launch (start us, length us, event | category | flops | bytes accessed | tf_op | source)
XLA Modules:
  0.0 380.6 jit_solution(5118960952709081886)
XLA Ops:
  6.5 2.5 reshape.288
  9.0 14.6 %all-to-all-start = ((f32[1,128,1024]{2,0,1:T(1,128)}), f32[1,128,1024]{2,0,1:T(1,128)S(1)}, u32[]{:S(2)}, u32[]{:S(2)}) async-start(f32[1,128,1024]{2,0,1:T(1,128)} %reshape.288), calls=%async_computation | async-start | bytes 1048576 | tf_op jit(solution)/shard_map/all_to_all | solution.py:137
  25.3 41.9 %all-reduce.66.cloned.1.call-done = f32[3,32,1024]{2,1,0:T(8,128)} async-done(((f32[3,32,1024]{2,1,0:T(8,128)}), f32[3,32,1024]{2,1,0:T(8,128)}) %all-reduce.66.cloned.1.call-update) | async-done | bytes 393232 | tf_op jit(solution)/shard_map/psum | solution.py:23
  70.7 1.8 copy.21
  72.4 10.6 %all-to-all-start.1 = ((f32[64,2,2048]{2,1,0:T(2,128)}), f32[64,2,2048]{2,1,0:T(2,128)S(1)}, u32[]{:S(2)}, u32[]{:S(2)}) async-start(f32[64,2,2048]{2,1,0:T(2,128)} %copy.21), calls=%async_computation.1 | async-start | bytes 2097152 | tf_op jit(solution)/shard_map/all_to_all | solution.py:35
  83.1 35.4 %all-reduce.68.cloned.1.call-done = f32[3,32,1024]{2,1,0:T(8,128)} async-done(((f32[3,32,1024]{2,1,0:T(8,128)}), f32[3,32,1024]{2,1,0:T(8,128)}) %all-reduce.68.cloned.1.call-update) | async-done | bytes 393232 | tf_op jit(solution)/shard_map/psum | solution.py:23
  118.7 76.7 %all-reduce.70.cloned.1.call-done = f32[3,32,1024]{2,1,0:T(8,128)} async-done(((f32[3,32,1024]{2,1,0:T(8,128)}), f32[3,32,1024]{2,1,0:T(8,128)}) %all-reduce.70.cloned.1.call-update) | async-done | bytes 393232 | tf_op jit(solution)/shard_map/psum | solution.py:23
  199.6 1.3 fusion.13
  200.9 1.3 convolution_subtract_fusion.1
  202.2 1.3 convolution_add_fusion.1
  204.6 4.6 %all_to_all.70 = f32[2,2,2,32,1024]{4,2,0,3,1:T(2,128)S(1)} all-to-all(f32[2,2,2,32,1024]{4,2,0,3,1:T(2,128)S(1)} %copy.26), channel_id=1, replica_groups=mesh['span_0'=2,'span_1'=4,'span_2'=8,'rows_0'=2,'rows_1'=2] {'rows_1'}, dimensions={1} | all-to-all | bytes 2097152 | tf_op jit(solution)/shard_map/all_to_all | solution.py:57
  210.3 4.4 %all-to-all-start.3 = ((f32[2,2,2,32,1024]{4,2,1,3,0:T(2,128)}), f32[2,2,2,32,1024]{4,2,1,3,0:T(2,128)}, u32[]{:S(2)}, u32[]{:S(2)}) async-start(f32[2,2,2,32,1024]{4,2,1,3,0:T(2,128)} %copy.27), calls=%async_computation.3 | async-start | bytes 2097152 | tf_op jit(solution)/shard_map/all_to_all | solution.py:57
  214.9 13.3 %all-gather.2.cloned.1.call-done = f32[128,3072]{1,0:T(8,128)} async-done(((f32[32,3072]{1,0:T(8,128)}), f32[128,3072]{1,0:T(8,128)}) %all-gather.2.cloned.1.call-update) | async-done | bytes 1572880 | tf_op jit(solution)/shard_map/all_gather | solution.py:73
  231.0 3.6 all-to-all-done.3
  234.7 1.8 copy.28
  239.1 2.1 multiply_add_fusion.11
  253.6 1.7 fusion.150
  255.3 1.9 fusion.151
  257.2 3.5 multiply_add_fusion.4
  269.5 4.6 %add_add_fusion = f32[2,128,1024]{2,1,0:T(8,128)S(1)} fusion(f32[2,127,1024]{2,1,0:T(8,128)} %get-tuple-element.38, f32[2,127,1024]{2,1,0:T(8,128)S(1)} %get-tuple-element.37, f32[2,128,1023]{2,1,0:T(8,128)S(1)} %get-tuple-element.36, f32[2,128,1023]{2,1,0:T(8,128)S(1)} %get-tuple-element.35, f32[2,128,1024]{2,1,0:T(8,128)S(1)} %get-tuple-element.7, ...), kind=kLoop, calls=%fused_computation.11 | loop fusion | flops 15204352 | bytes 27226120 | tf_op jit(solution)/shard_map/add | solution.py:115
  275.0 17.0 %all_to_all.71 = f32[2,128,1024]{2,0,1:T(2,128)S(1)} all-to-all(f32[2,128,1024]{2,0,1:T(2,128)S(1)} %copy.29), channel_id=1, replica_groups=mesh['span_0'=2,'span_1'=4,'span_2'=8,'rows_0'=2,'rows_1'=2] {'rows_0','..., dimensions={1} | all-to-all | bytes 2097152 | tf_op jit(solution)/shard_map/all_to_all | solution.py:177
  300.2 43.1 %all_to_all.72 = f32[1,128,2048]{2,0,1:T(1,128)S(1)} all-to-all(f32[1,128,2048]{2,0,1:T(1,128)S(1)} %copy.35), channel_id=1, replica_groups=mesh['span_0'=2,'span_1'=4,'span_2'=8,'rows_0'=2,'rows_1'=2] {'span_0','..., dimensions={1} | all-to-all | bytes 2097152 | tf_op jit(solution)/shard_map/all_to_all | solution.py:35
  343.2 2.5 reduce.1
  348.5 24.2 %all_to_all.73 = f32[64,2,1024]{2,1,0:T(2,128)S(1)} all-to-all(f32[64,2,1024]{2,1,0:T(2,128)S(1)} %copy.38), channel_id=1, replica_groups=mesh['span_0'=2,'span_1'=4,'span_2'=8,'rows_0'=2,'rows_1'=2] {'span_0','..., dimensions={0} | all-to-all | bytes 1048576 | tf_op jit(solution)/shard_map/all_to_all | solution.py:200
  (99 shorter events, 49.9 us)
Async XLA Ops:
  6.5 17.9 %copy-start.1 = (f32[1,3,32,1024]{3,2,1,0:T(8,128)S(1)}, f32[1,3,32,1024]{3,2,1,0:T(8,128)}, u32[]{:S(2)}) copy-start(f32[1,3,32,1024]{3,2,1,0:T(8,128)} %param.4) | copy-start | bytes 1179652
  9.0 58.2 %all-to-all-start = ((f32[1,128,1024]{2,0,1:T(1,128)}), f32[1,128,1024]{2,0,1:T(1,128)S(1)}, u32[]{:S(2)}, u32[]{:S(2)}) async-start(f32[1,128,1024]{2,0,1:T(1,128)} %reshape.288), calls=%async_computation | async-start | bytes 1048576 | tf_op jit(solution)/shard_map/all_to_all | solution.py:137
  23.7 43.5 %all-reduce.66.cloned.1.call-start = ((), (), s32[]{:S(2)}) async-start(), calls=%async_computation.7 | async-start | bytes 786432 | tf_op jit(solution)/shard_map/psum | solution.py:23
  25.2 93.2 %all-reduce.68.cloned.1.call-start = ((), (), s32[]{:S(2)}) async-start(), calls=%async_computation.8 | async-start | bytes 786432 | tf_op jit(solution)/shard_map/psum | solution.py:23
  72.4 125.0 %all-to-all-start.1 = ((f32[64,2,2048]{2,1,0:T(2,128)}), f32[64,2,2048]{2,1,0:T(2,128)S(1)}, u32[]{:S(2)}, u32[]{:S(2)}) async-start(f32[64,2,2048]{2,1,0:T(2,128)} %copy.21), calls=%async_computation.1 | async-start | bytes 2097152 | tf_op jit(solution)/shard_map/all_to_all | solution.py:35
  83.0 112.4 %all-reduce.70.cloned.1.call-start = ((), (), s32[]{:S(2)}) async-start(), calls=%async_computation.9 | async-start | bytes 786432 | tf_op jit(solution)/shard_map/psum | solution.py:23
  118.5 109.7 %all-gather.2.cloned.1.call-start = ((), (), s32[]{:S(2)}) async-start(), calls=%async_computation.10 | async-start | bytes 1966080 | tf_op jit(solution)/shard_map/all_gather | solution.py:73
  210.3 24.4 %all-to-all-start.3 = ((f32[2,2,2,32,1024]{4,2,1,3,0:T(2,128)}), f32[2,2,2,32,1024]{4,2,1,3,0:T(2,128)}, u32[]{:S(2)}, u32[]{:S(2)}) async-start(f32[2,2,2,32,1024]{4,2,1,3,0:T(2,128)} %copy.27), calls=%async_computation.3 | async-start | bytes 2097152 | tf_op jit(solution)/shard_map/all_to_all | solution.py:57
  228.2 2.5 copy-start
Sparse Core Ops, SparseCore 0:
  27.1 40.0 all-reduce.65
  69.6 48.7 all-reduce.67
  120.8 74.6 all-reduce.69
  197.4 30.7 all-gather.1
where the time goes:
time: 387 us; the launch traced here: 381 us
  waiting for transfers between devices  171 us (44%)
  blocking collectives  88.9 us (23%)
  local copies, waits for them, and re-layouts  32.6 us (8%)
  other arithmetic  30.6 us (8%)
  starting transfers between devices  30 us (8%)
  between operations  14.8 us (4%)
  matrix products  12.8 us (3%)
    psum x3, waiting for transfers between devices, spread(): x = lax.psum(x, axis)  154 us
    all_to_all x1, blocking collectives, in_one_piece(): lax.all_to_all(both, axis, split_axis=split_dim, concat_axis=concat_dim,...  43.1 us
    all_to_all x1, blocking collectives, on_device(): lax.all_to_all(gathered_rows, SPAN, split_axis=0, concat_axis=1, tiled=True)  24.2 us
    add x13, other arithmetic, chebyshev(): ratio_next * ratio_now * direction  18.3 us
    all_to_all x1, blocking collectives, on_device(): lax.all_to_all(solved_mine, ROWS, split_axis=1, concat_axis=0, tiled=True)  17 us
    all_to_all x1, starting transfers between devices, on_device(): lax.all_to_all(merged, SPAN, split_axis=1, concat_axis=0, tiled=True)  14.6 us
    all_gather x1, waiting for transfers between devices, side_by_side(): lax.all_gather(both, axis, axis=dim, tiled=True)  13.3 us
    all_to_all x1, starting transfers between devices, in_one_piece(): lax.all_to_all(both, axis, split_axis=split_dim, concat_axis=concat_dim,...  10.6 us
  transfers between devices with their start and end apart: 7, of which 5 were waited for; matrix products, arithmetic and copies ran while one was open for 5% of the time, Pallas kernels for 0%

commit v1 on v0

v1 whole, which is shorter than its diff:
```python
import math

import jax
import jax.numpy as jnp
import ml_dtypes
import numpy as np
from jax import lax
from jax.experimental import pallas as pl
from jax.experimental.pallas import tpu as pltpu
from jax.sharding import PartitionSpec as P

MESH = pl.DeviceIdType.MESH
F32 = jnp.float32
BF16 = jnp.bfloat16

SWEEPS = 2
STEPS = 8
LOWER_BOUND = 0.02
UPPER_BOUND = 2.0
CENTER = (UPPER_BOUND + LOWER_BOUND) / 2.0
HALF_WIDTH = (UPPER_BOUND - LOWER_BOUND) / 2.0

NZ = 256
SPAN = 64
ROWS = 4
CELL_ROWS = NZ * 4
LANES = 128


def mode_numbers():
    slot = np.arange(NZ)
    return np.where(slot <= NZ // 2, slot, slot - NZ // 2), slot <= NZ // 2


def transform_tables():
    modes, is_real = mode_numbers()
    points = np.arange(NZ)
    angle = 2.0 * np.pi * ((modes[:, None] * points[None, :]) % NZ) / NZ
    forward = np.where(is_real[:, None], np.cos(angle), -np.sin(angle))
    weight = np.where((modes == 0) | (modes == NZ // 2), 1.0, 2.0)
    inverse = (forward * weight[:, None] / NZ).T
    pieces = []
    for table in (forward, inverse):
        high = table.astype(ml_dtypes.bfloat16)
        low = (table - high.astype(np.float64)).astype(ml_dtypes.bfloat16)
        pieces += [high, low]
    return np.stack(pieces)


def eigen_table():
    modes, _ = mode_numbers()
    return (2.0 - 2.0 * np.cos(2.0 * np.pi * modes / NZ)).astype(np.float32)


def step_table():
    sigma = CENTER / HALF_WIDTH
    keep, add = [], []
    for _ in range(SWEEPS):
        ratio = 1.0 / sigma
        for _ in range(STEPS):
            ratio_next = 1.0 / (2.0 * sigma - ratio)
            keep.append(ratio_next * ratio)
            add.append(2.0 * ratio_next / HALF_WIDTH)
            ratio = ratio_next
        keep[-1], add[-1] = 0.0, 1.0 / CENTER
    return np.array([keep, add], np.float32)


def transform(high, low, x):
    x_high = x.astype(BF16)
    x_low = (x - x_high.astype(F32)).astype(BF16)
    out = jnp.dot(high, x_high, preferred_element_type=F32)
    out += jnp.dot(high, x_low, preferred_element_type=F32)
    out += jnp.dot(low, x_high, preferred_element_type=F32)
    return out


def gathered(ref):
    return jnp.concatenate([ref[pl.ds(q, NZ, stride=4), :] for q in range(4)], axis=1)


def scattered(ref, value):
    for q in range(4):
        ref[pl.ds(q, NZ, stride=4), :] = value[:, q * LANES : (q + 1) * LANES]


def kernel(
    x_ref,
    g_ref,
    owner_ref,
    eigen_ref,
    step_ref,
    table_ref,
    o_ref,
    cells_out,
    cells_in,
    modes_out,
    plane_in,
    plane_out,
    modes_in,
    points_out,
    points_in,
    masked,
    part_x,
    sum_x,
    part_y,
    sum_y,
    part_z,
    geo,
    coef,
    zed,
    acc,
    ways,
    send_sem,
    recv_sem,
    geo_send,
    geo_recv,
    self_sem,
):
    span = lax.axis_index("span")
    row = lax.axis_index("rows")
    zi = lax.rem(span, 8)
    xi = lax.rem(lax.div(span, 8), 4)
    yh = lax.div(span, 32)
    yl = lax.div(row, 2)
    core = lax.rem(row, 2)
    mine = span * 4 + row
    place = 64 * row + span

    def span_peer(d):
        dz, dx, dy = lax.rem(d, 8), lax.rem(lax.div(d, 8), 4), lax.div(d, 32)
        return lax.rem(yh + dy, 2) * 32 + lax.rem(xi + dx, 4) * 8 + lax.rem(zi + dz, 8)

    def any_peer(d):
        dc, dl = lax.rem(d, 2), lax.rem(lax.div(d, 2), 2)
        return span_peer(lax.div(d, 4)), lax.rem(yl + dl, 2) * 2 + lax.rem(core + dc, 2)

    def rows_of(ref, start, size, unit):
        return ref.at[pl.ds(pl.multiple_of(start, unit), size)]

    def push(src, dst, sems, peer):
        pltpu.make_async_remote_copy(
            src_ref=src,
            dst_ref=dst,
            send_sem=sems[0],
            recv_sem=sems[1],
            device_id=peer,
            device_id_type=MESH,
        ).start()

    def await_rows(ref, count, sem):
        pltpu.make_async_copy(ref.at[pl.ds(0, count)], ref.at[pl.ds(0, count)], sem).wait()

    barrier = pltpu.get_barrier_semaphore()

    @pl.loop(1, SPAN)
    def _(d):
        pl.semaphore_signal(barrier, inc=1, device_id=(span_peer(d), row), device_id_type=MESH)

    for d in range(1, ROWS):
        pl.semaphore_signal(
            barrier, inc=1, device_id=(span, lax.rem(row + d, ROWS)), device_id_type=MESH
        )

    own = owner_ref[0] == span
    for x_to in range(4):
        for y_to in range(2):
            tile_row, half = divmod(y_to * 4 + x_to, 2)
            for z_to in range(8):
                for comp in range(3):
                    piece = g_ref[comp, 8 * tile_row + 4 * half : 8 * tile_row + 4 * half + 4,
                                  z_to * LANES : (z_to + 1) * LANES]
                    at = ((x_to * 2 + y_to) * 8 + z_to) * 12 + comp * 4
                    masked[at : at + 4, :] = jnp.where(own, piece, jnp.zeros_like(piece))

    for to in range(SPAN):
        rows_at, cols_at = 4 * (to // 8), LANES * (to % 8)
        for j in range(4):
            cells_out[16 * to + 4 * j : 16 * to + 4 * j + 4, :] = x_ref[
                j, rows_at : rows_at + 4, cols_at : cols_at + LANES
            ]

    pl.semaphore_wait(barrier, SPAN - 1 + ROWS - 1)

    def geo_sems(k):
        return geo_send.at[k], geo_recv.at[k]

    def span_at(y, x, z):
        return y * 32 + x * 8 + z

    for d in range(1, 4):
        to = lax.rem(xi + d, 4)
        push(
            rows_of(masked, to * 192, 192, 8),
            rows_of(part_x, xi * 192, 192, 8),
            geo_sems(0),
            (span_at(yh, to, zi), row),
        )

    def sems(k):
        return send_sem.at[k], recv_sem.at[k]

    @pl.loop(1, SPAN)
    def _(d):
        to = span_peer(d)
        push(
            rows_of(cells_out, to * 16, 16, 16),
            rows_of(cells_in, span * 16, 16, 16),
            sems(0),
            (to, row),
        )

    cells_in[pl.ds(pl.multiple_of(span * 16, 16), 16), :] = cells_out[
        pl.ds(pl.multiple_of(span * 16, 16), 16), :
    ]
    part_x[pl.ds(pl.multiple_of(xi * 192, 8), 192), :] = masked[
        pl.ds(pl.multiple_of(xi * 192, 8), 192), :
    ]

    await_rows(part_x, 576, geo_recv.at[0])
    sum_x[...] = part_x[0:192] + part_x[192:384] + part_x[384:576] + part_x[576:768]
    push(
        rows_of(sum_x, (1 - yh) * 96, 96, 8),
        part_y,
        geo_sems(1),
        (span_at(1 - yh, xi, zi), row),
    )
    await_rows(part_y, 96, geo_recv.at[1])
    sum_y[...] = part_y[...] + sum_x[pl.ds(pl.multiple_of(yh * 96, 8), 96), :]
    for d in range(1, 8):
        to = lax.rem(zi + d, 8)
        push(
            rows_of(sum_y, to * 12, 12, 4),
            rows_of(part_z, zi * 16, 12, 4),
            geo_sems(2),
            (span_at(yh, xi, to), row),
        )
    keep_z = pltpu.make_async_copy(
        rows_of(sum_y, zi * 12, 12, 4), rows_of(part_z, zi * 16, 12, 4), self_sem.at[0]
    )
    keep_z.start()
    keep_z.wait()
    await_rows(part_z, 84, geo_recv.at[2])
    total = part_z[0:12]
    for d in range(1, 8):
        total = total + part_z[16 * d : 16 * d + 12]
    sum_y_own = masked.at[pl.ds(768, 12)]
    masked[768:780, :] = total

    here = 12 * place
    for d in range(1, 8):
        push(
            sum_y_own,
            rows_of(geo, here, 12, 4),
            geo_sems(3),
            (span_at(yh, xi, lax.rem(zi + d, 8)), row),
        )
    keep_geo = pltpu.make_async_copy(sum_y_own, rows_of(geo, here, 12, 4), self_sem.at[1])
    keep_geo.start()
    keep_geo.wait()

    await_rows(cells_in, 1008, recv_sem.at[0])
    scattered(modes_out, transform(table_ref[0], table_ref[1], gathered(cells_in)))

    @pl.loop(1, NZ)
    def _(d):
        to_span, to_row = any_peer(d)
        push(
            rows_of(modes_out, (to_span * 4 + to_row) * 4, 4, 4),
            rows_of(plane_in, place * 4, 4, 4),
            sems(1),
            (to_span, to_row),
        )

    keep_plane = pltpu.make_async_copy(
        rows_of(modes_out, mine * 4, 4, 4), rows_of(plane_in, place * 4, 4, 4), self_sem.at[2]
    )
    keep_plane.start()
    keep_plane.wait()

    def block(r, y, x):
        return rows_of(geo, 12 * (64 * r + 32 * y + 8 * x), 96, 8)

    await_rows(geo, 84, geo_recv.at[3])
    for d in range(1, 4):
        y_to, l_to = lax.rem(yh + d // 2, 2), lax.rem(yl + d % 2, 2)
        push(
            block(row, yh, xi),
            block(row, yh, xi),
            geo_sems(4),
            (span_at(y_to, xi, zi), 2 * l_to + core),
        )
    await_rows(geo, 288, geo_recv.at[4])
    for d in range(1, 4):
        to = lax.rem(xi + d, 4)
        for l in range(2):
            for y in range(2):
                push(
                    block(2 * l + core, y, xi),
                    block(2 * l + core, y, xi),
                    geo_sems(5),
                    (span_at(yh, to, zi), row),
                )
    await_rows(geo, 1152, geo_recv.at[5])
    for l in range(2):
        push(
            rows_of(geo, 768 * (2 * l + core), 768, 8),
            rows_of(geo, 768 * (2 * l + core), 768, 8),
            geo_sems(6),
            (span, 2 * yl + 1 - core),
        )
    await_rows(geo, 1536, geo_recv.at[6])

    await_rows(plane_in, 1020, recv_sem.at[1])

    eigen = eigen_ref[mine]
    lane = lax.broadcasted_iota(jnp.int32, (8, LANES), 1)
    sub = lax.broadcasted_iota(jnp.int32, (8, LANES), 0)
    first_lane, last_lane = lane == 0, lane == LANES - 1
    first_sub, last_sub = sub == 0, sub == 7

    def face(comp, x, q, z):
        return geo[pl.ds(12 * (8 * x + z) + 4 * comp + q, 8, stride=384), :]

    def slot(i, z):
        return pl.ds(pl.multiple_of((i * 8 + z) * 8, 8), 8)

    def way(parity, i, z):
        return pl.ds(pl.multiple_of(parity * 1152 + ((i + 1) * 8 + z) * 8, 8), 8)

    def to_left(v):
        return pltpu.roll(v, LANES - 1, 1)

    def to_right(v):
        return pltpu.roll(v, 1, 1)

    for x in range(4):
        for q in range(4):
            i = 4 * x + q
            west = [face(0, x, q, z) for z in range(8)]
            moved = [to_left(w) for w in west] + [jnp.zeros((8, LANES), F32)]
            for z in range(8):
                north = face(1, x, q, z)
                if i < 15:
                    south = face(1, (i + 1) // 4, (i + 1) % 4, z)
                else:
                    south = jnp.where(last_sub, 0.0, pltpu.roll(face(1, 0, 0, z), 7, 0))
                east = jnp.where(last_lane, moved[z + 1], moved[z])
                inverse = 1.0 / (west[z] + east + north + south + eigen * face(2, x, q, z))
                west_in = jnp.where(first_lane, 0.0, west[z]) if z == 0 else west[z]
                north_in = jnp.where(first_sub, 0.0, north) if i == 0 else north
                coef[0, slot(i, z), :] = west_in * inverse
                coef[1, slot(i, z), :] = east * inverse
                coef[2, slot(i, z), :] = north_in * inverse
                coef[3, slot(i, z), :] = south * inverse
                value = plane_in[pl.ds(4 * (8 * x + z) + q, 8, stride=128), :] * inverse
                zed[slot(i, z), :] = value
                way_0 = value * (1.0 / CENTER)
                ways[way(0, i, z), :] = way_0
                acc[slot(i, z), :] = jnp.zeros((8, LANES), F32)
                if i == 15:
                    ways[way(0, -1, z), :] = pltpu.roll(way_0, 1, 0)
                if i == 0:
                    ways[way(0, 16, z), :] = pltpu.roll(way_0, 7, 0)

    def one_step(step, carry):
        now = lax.rem(step, 2)
        later = 1 - now
        keep, add = step_ref[0, step], step_ref[1, step]

        def one_row(i, carry):
            mid = [ways[way(now, i, z), :] for z in range(8)]
            right = [to_right(m) for m in mid]
            left = [to_left(m) for m in mid]
            for z in range(8):
                from_west = jnp.where(first_lane, right[z - 1], right[z]) if z else right[z]
                from_east = jnp.where(last_lane, left[z + 1], left[z]) if z < 7 else left[z]
                flow = coef[0, slot(i, z), :] * from_west + coef[1, slot(i, z), :] * from_east
                flow += coef[2, slot(i, z), :] * ways[way(now, i - 1, z), :]
                flow += coef[3, slot(i, z), :] * ways[way(now, i + 1, z), :]
                value = zed[slot(i, z), :] - mid[z] + flow
                zed[slot(i, z), :] = value
                acc[slot(i, z), :] += mid[z]
                ways[way(later, i, z), :] = keep * mid[z] + add * value
            return carry

        lax.fori_loop(0, 16, one_row, 0)
        for z in range(8):
            ways[way(later, -1, z), :] = pltpu.roll(ways[way(later, 15, z), :], 1, 0)
            ways[way(later, 16, z), :] = pltpu.roll(ways[way(later, 0, z), :], 7, 0)
        return carry

    last = SWEEPS * STEPS - 1
    lax.fori_loop(0, last, one_step, 0)
    for x in range(4):
        for q in range(4):
            i = 4 * x + q
            for z in range(8):
                plane_out[pl.ds(4 * (8 * x + z) + q, 8, stride=128), :] = (
                    acc[slot(i, z), :] + ways[way(last % 2, i, z), :]
                )

    @pl.loop(1, NZ)
    def _(d):
        to_span, to_row = any_peer(d)
        push(
            rows_of(plane_out, (64 * to_row + to_span) * 4, 4, 4),
            rows_of(modes_in, mine * 4, 4, 4),
            sems(2),
            (to_span, to_row),
        )

    keep_modes = pltpu.make_async_copy(
        rows_of(plane_out, place * 4, 4, 4), rows_of(modes_in, mine * 4, 4, 4), self_sem.at[3]
    )
    keep_modes.start()
    keep_modes.wait()
    await_rows(modes_in, 1020, recv_sem.at[2])
    scattered(points_out, transform(table_ref[2], table_ref[3], gathered(modes_in)))

    @pl.loop(1, SPAN)
    def _(d):
        to = span_peer(d)
        push(
            rows_of(points_out, to * 16, 16, 16),
            rows_of(points_in, span * 16, 16, 16),
            sems(3),
            (to, row),
        )

    points_in[pl.ds(pl.multiple_of(span * 16, 16), 16), :] = points_out[
        pl.ds(pl.multiple_of(span * 16, 16), 16), :
    ]
    await_rows(points_in, 1008, recv_sem.at[3])
    for source in range(SPAN):
        rows_at, cols_at = 4 * (source // 8), LANES * (source % 8)
        for j in range(4):
            o_ref[j, rows_at : rows_at + 4, cols_at : cols_at + LANES] = points_in[
                16 * source + 4 * j : 16 * source + 4 * j + 4, :
            ]

    await_rows(cells_out, 1008, send_sem.at[0])
    await_rows(modes_out, 1020, send_sem.at[1])
    await_rows(plane_out, 1020, send_sem.at[2])
    await_rows(points_out, 1008, send_sem.at[3])
    for k, count in enumerate((576, 96, 84, 84, 288, 1152, 1536)):
        await_rows(geo, count, geo_send.at[k])


def on_device(pressure_source, geometry, owner, eigen, steps, tables):
    vmem = pl.BlockSpec(memory_space=pltpu.VMEM)
    smem = pl.BlockSpec(memory_space=pltpu.SMEM)
    cells = pltpu.VMEM((CELL_ROWS, LANES), F32)
    return pl.pallas_call(
        kernel,
        out_shape=jax.ShapeDtypeStruct(pressure_source.shape, F32),
        in_specs=[vmem, vmem, smem, smem, smem, vmem],
        out_specs=vmem,
        scratch_shapes=[cells] * 8
        + [
            pltpu.VMEM((784, LANES), F32),
            pltpu.VMEM((768, LANES), F32),
            pltpu.VMEM((192, LANES), F32),
            pltpu.VMEM((96, LANES), F32),
            pltpu.VMEM((96, LANES), F32),
            pltpu.VMEM((128, LANES), F32),
            pltpu.VMEM((3072, LANES), F32),
            pltpu.VMEM((4, CELL_ROWS, LANES), F32),
            cells,
            cells,
            pltpu.VMEM((2304, LANES), F32),
            pltpu.SemaphoreType.DMA((4,)),
            pltpu.SemaphoreType.DMA((4,)),
            pltpu.SemaphoreType.DMA((7,)),
            pltpu.SemaphoreType.DMA((7,)),
            pltpu.SemaphoreType.DMA((4,)),
        ],
        compiler_params=pltpu.CompilerParams(
            collective_id=0, has_side_effects=True, vmem_limit_bytes=48 * 2**20
        ),
    )(pressure_source, geometry[0], owner, eigen, steps, tables)


def solution(mesh):
    eigen, steps, tables = eigen_table(), step_table(), transform_tables()

    def whole(pressure_source, geometry, owner):
        return jax.shard_map(
            on_device,
            mesh=mesh,
            in_specs=(P("span", "rows", None), P("span", None, "rows", None), P(), P(), P(), P()),
            out_specs=P("span", "rows", None),
            check_vma=False,
        )(pressure_source, geometry, owner, eigen, steps, tables)

    return whole
```

time: 387 us -> 129 us (0.33); the launches traced: 381 us -> 128 us
  waiting for transfers between devices: 171 us -> 0 us
  Pallas kernels: 0 us -> 123 us
  blocking collectives: 88.9 us -> 0 us
  other arithmetic: 30.6 us -> 0 us
  starting transfers between devices: 30 us -> 0 us
  local copies, waits for them, and re-layouts: 32.6 us -> 4.54 us
  between operations: 14.8 us -> 0.69 us
  matrix products: 12.8 us -> 0 us
    psum x3 -> x0, waiting for transfers between devices: 154 us -> none  [spread(): x = lax.psum(x, axis)]
    pallas_call x0 -> x1, Pallas kernels: none -> 123 us  [on_device(): pl.pallas_call(kernel, out_shape=jax.ShapeDtypeStruct(pressure_source.sha...]
    all_to_all x4 -> x0, blocking collectives: 88.9 us -> none  [the longest x1 43.1 us: in_one_piece(): lax.all_to_all(both, axis, split_axis=split_dim, concat_axis=concat_dim,...]
    all_to_all x3 -> x0, starting transfers between devices: 29.6 us -> none  [the longest x1 14.6 us: on_device(): lax.all_to_all(merged, SPAN, split_axis=1, concat_axis=0, tiled=True)]
    add x16 -> x0, other arithmetic: 22.9 us -> none  [the longest x13 18.3 us: chebyshev(): ratio_next * ratio_now * direction]
    slice x37 -> x0, local copies, waits for them, and re-layouts: 17.3 us -> none  [the longest x15 7.07 us: apply_faces(): left_cols = jnp.concatenate([zero_col, planes[:, :, :-1]], axis=2)]
    all_gather x1 -> x0, waiting for transfers between devices: 13.3 us -> none  [side_by_side(): lax.all_gather(both, axis, axis=dim, tiled=True)]
    dot_general x12 -> x0, matrix products: 12.8 us -> none  [the longest x1 1.32 us: on_device(): jnp.einsum('kj,jyc->kyc', forward_cos, imag_part, precision=HIGHEST)]
  transfers between devices with their start and end apart: 7 -> 0, of which waited for: 5 -> 0; matrix products, arithmetic and copies ran while one was open for 5% -> 0% of each run, Pallas kernels for 0% -> 0%
where the time goes in v1:
time: 129 us; the launch traced here: 128 us
  Pallas kernels  123 us (95%)
  local copies, waits for them, and re-layouts  4.54 us (4%)
    pallas_call x1, Pallas kernels, on_device(): pl.pallas_call(kernel, out_shape=jax.ShapeDtypeStruct(pressure_source.sha...  123 us
    unnamed x11, local copies, waits for them, and re-layouts  4.54 us

profile of v1, /device:TPU:6, one launch (start us, length us, event | category | flops | bytes accessed | tf_op | source)
XLA Modules:
  0.0 128.1 jit_solution(6142215128886622972)
XLA Ops:
  0.0 0.0 copy-start.4
  0.7 0.0 copy-start.3
  0.7 0.0 copy-done.4
  0.7 0.7 copy-done.3
  1.4 0.0 copy-start
  1.4 1.0 copy-done
  2.4 0.0 copy-start.1
  2.4 1.0 copy-done.1
  3.4 0.0 copy-start.2
  3.4 1.0 copy-done.2
  4.4 122.8 %shard_map.64 = f32[4,32,1024]{2,1,0:T(8,128)S(1)} custom-call(f32[4,32,1024]{2,1,0:T(8,128)S(1)} %copy-done, f32[3,32,1024]{2,1,0:T(8,128)S(1)} %bitcast.1, s32[1]{0:T(128)S(6)} %copy.8.owner_ref, f32[256]{0:T(256)S(1)} %copy-done.4, f32[2,16]{1,0:T(2,128)S(1)} %copy-done.3, bf16[4,256,256]{2,1,0:T(8,128)(2,1)S(1)} %copy-done.1), custom_call_target="tpu_custom_call" | custom-call | tf_op jit(solution)/shard_map/pallas_call | solution.py:454
  127.3 0.8 copy.9
Async XLA Ops:
  0.0 0.7 copy-start.4
  0.7 0.7 copy-start.3
  1.4 1.0 copy-start
  2.4 1.0 copy-start.1
  3.4 1.0 copy-start.2

commit v2 on v1

--- a/solution.py
+++ b/solution.py
@@ -85,13 +85,16 @@
 
 
 def kernel(
-    x_ref,
-    g_ref,
+    x_hbm,
+    g_hbm,
     owner_ref,
     eigen_ref,
     step_ref,
+    table_hbm,
+    o_ref,
+    x_ref,
+    g_ref,
     table_ref,
-    o_ref,
     cells_out,
     cells_in,
     modes_out,
@@ -110,7 +113,9 @@
     coef,
     zed,
     acc,
-    ways,
+    way_a,
+    way_b,
+    in_sem,
     send_sem,
     recv_sem,
     geo_send,
@@ -151,6 +156,15 @@
     def await_rows(ref, count, sem):
         pltpu.make_async_copy(ref.at[pl.ds(0, count)], ref.at[pl.ds(0, count)], sem).wait()
 
+    fetch = [
+        pltpu.make_async_copy(src, dst, in_sem.at[k])
+        for k, (src, dst) in enumerate(
+            ((x_hbm, x_ref), (g_hbm, g_ref), (table_hbm, table_ref))
+        )
+    ]
+    for copy in fetch:
+        copy.start()
+
     barrier = pltpu.get_barrier_semaphore()
 
     @pl.loop(1, SPAN)
@@ -162,6 +176,7 @@
             barrier, inc=1, device_id=(span, lax.rem(row + d, ROWS)), device_id_type=MESH
         )
 
+    fetch[1].wait()
     own = owner_ref[0] == span
     for x_to in range(4):
         for y_to in range(2):
@@ -173,6 +188,7 @@
                     at = ((x_to * 2 + y_to) * 8 + z_to) * 12 + comp * 4
                     masked[at : at + 4, :] = jnp.where(own, piece, jnp.zeros_like(piece))
 
+    fetch[0].wait()
     for to in range(SPAN):
         rows_at, cols_at = 4 * (to // 8), LANES * (to % 8)
         for j in range(4):
@@ -239,8 +255,8 @@
         rows_of(sum_y, zi * 12, 12, 4), rows_of(part_z, zi * 16, 12, 4), self_sem.at[0]
     )
     keep_z.start()
+    await_rows(part_z, 84, geo_recv.at[2])
     keep_z.wait()
-    await_rows(part_z, 84, geo_recv.at[2])
     total = part_z[0:12]
     for d in range(1, 8):
         total = total + part_z[16 * d : 16 * d + 12]
@@ -257,9 +273,9 @@
         )
     keep_geo = pltpu.make_async_copy(sum_y_own, rows_of(geo, here, 12, 4), self_sem.at[1])
     keep_geo.start()
-    keep_geo.wait()
 
     await_rows(cells_in, 1008, recv_sem.at[0])
+    fetch[2].wait()
     scattered(modes_out, transform(table_ref[0], table_ref[1], gathered(cells_in)))
 
     @pl.loop(1, NZ)
@@ -276,12 +292,12 @@
         rows_of(modes_out, mine * 4, 4, 4), rows_of(plane_in, place * 4, 4, 4), self_sem.at[2]
     )
     keep_plane.start()
-    keep_plane.wait()
 
     def block(r, y, x):
         return rows_of(geo, 12 * (64 * r + 32 * y + 8 * x), 96, 8)
 
     await_rows(geo, 84, geo_recv.at[3])
+    keep_geo.wait()
     for d in range(1, 4):
         y_to, l_to = lax.rem(yh + d // 2, 2), lax.rem(yl + d % 2, 2)
         push(
@@ -312,6 +328,7 @@
     await_rows(geo, 1536, geo_recv.at[6])
 
     await_rows(plane_in, 1020, recv_sem.at[1])
+    keep_plane.wait()
 
     eigen = eigen_ref[mine]
     lane = lax.broadcasted_iota(jnp.int32, (8, LANES), 1)
@@ -323,10 +340,7 @@
         return geo[pl.ds(12 * (8 * x + z) + 4 * comp + q, 8, stride=384), :]
 
     def slot(i, z):
-        return pl.ds(pl.multiple_of((i * 8 + z) * 8, 8), 8)
-
-    def way(parity, i, z):
-        return pl.ds(pl.multiple_of(parity * 1152 + ((i + 1) * 8 + z) * 8, 8), 8)
+        return pl.ds((i * 8 + z) * 8, 8)
 
     def to_left(v):
         return pltpu.roll(v, LANES - 1, 1)
@@ -355,50 +369,64 @@
                 coef[3, slot(i, z), :] = south * inverse
                 value = plane_in[pl.ds(4 * (8 * x + z) + q, 8, stride=128), :] * inverse
                 zed[slot(i, z), :] = value
-                way_0 = value * (1.0 / CENTER)
-                ways[way(0, i, z), :] = way_0
+                way_a[slot(i, z), :] = value * (1.0 / CENTER)
                 acc[slot(i, z), :] = jnp.zeros((8, LANES), F32)
-                if i == 15:
-                    ways[way(0, -1, z), :] = pltpu.roll(way_0, 1, 0)
-                if i == 0:
-                    ways[way(0, 16, z), :] = pltpu.roll(way_0, 7, 0)
-
-    def one_step(step, carry):
-        now = lax.rem(step, 2)
-        later = 1 - now
-        keep, add = step_ref[0, step], step_ref[1, step]
-
-        def one_row(i, carry):
-            mid = [ways[way(now, i, z), :] for z in range(8)]
-            right = [to_right(m) for m in mid]
-            left = [to_left(m) for m in mid]
-            for z in range(8):
-                from_west = jnp.where(first_lane, right[z - 1], right[z]) if z else right[z]
-                from_east = jnp.where(last_lane, left[z + 1], left[z]) if z < 7 else left[z]
-                flow = coef[0, slot(i, z), :] * from_west + coef[1, slot(i, z), :] * from_east
-                flow += coef[2, slot(i, z), :] * ways[way(now, i - 1, z), :]
-                flow += coef[3, slot(i, z), :] * ways[way(now, i + 1, z), :]
-                value = zed[slot(i, z), :] - mid[z] + flow
-                zed[slot(i, z), :] = value
-                acc[slot(i, z), :] += mid[z]
-                ways[way(later, i, z), :] = keep * mid[z] + add * value
-            return carry
-
-        lax.fori_loop(0, 16, one_row, 0)
+
+    lanes = lax.broadcasted_iota(jnp.int32, (64, LANES), 1)
+    first_lanes, last_lanes = lanes == 0, lanes == LANES - 1
+
+    def line(i):
+        return pl.ds(64 * i, 64)
+
+    def turned(v, shift):
+        return jnp.concatenate(
+            [pltpu.roll(v[8 * z : 8 * z + 8], shift, 0) for z in range(8)], axis=0
+        )
+
+    def residuals(ways, done):
+        above, mid = turned(ways[line(15), :], 1), ways[line(0), :]
+        for i in range(16):
+            below = ways[line(i + 1), :] if i < 15 else turned(ways[line(0), :], 7)
+            right, left = to_right(mid), to_left(mid)
+            from_west = jnp.where(
+                first_lanes, jnp.concatenate([right[56:], right[:56]], axis=0), right
+            )
+            from_east = jnp.where(
+                last_lanes, jnp.concatenate([left[8:], left[:8]], axis=0), left
+            )
+            flow = coef[0, line(i), :] * from_west + coef[1, line(i), :] * from_east
+            flow += coef[2, line(i), :] * above + coef[3, line(i), :] * below
+            done(i, mid, zed[line(i), :] - mid + flow)
+            above, mid = mid, below
+
+    def two_steps(pair, carry):
+        keep_a, add_a = step_ref[0, 2 * pair], step_ref[1, 2 * pair]
+        keep_b, add_b = step_ref[0, 2 * pair + 1], step_ref[1, 2 * pair + 1]
+
+        def first_done(i, mid, value):
+            zed[line(i), :] = value
+            way_b[line(i), :] = keep_a * mid + add_a * value
+
+        def second_done(i, mid, value):
+            zed[line(i), :] = value
+            acc[line(i), :] += way_a[line(i), :] + mid
+            way_a[line(i), :] = keep_b * mid + add_b * value
+
+        residuals(way_a, first_done)
+        residuals(way_b, second_done)
+        return carry
+
+    last = SWEEPS * STEPS - 2
+    lax.fori_loop(0, last // 2, two_steps, 0)
+    keep, add = step_ref[0, last], step_ref[1, last]
+
+    def last_done(i, mid, value):
+        total = acc[line(i), :] + mid + (keep * mid + add * value)
+        x, q = divmod(i, 4)
         for z in range(8):
-            ways[way(later, -1, z), :] = pltpu.roll(ways[way(later, 15, z), :], 1, 0)
-            ways[way(later, 16, z), :] = pltpu.roll(ways[way(later, 0, z), :], 7, 0)
-        return carry
-
-    last = SWEEPS * STEPS - 1
-    lax.fori_loop(0, last, one_step, 0)
-    for x in range(4):
-        for q in range(4):
-            i = 4 * x + q
-            for z in range(8):
-                plane_out[pl.ds(4 * (8 * x + z) + q, 8, stride=128), :] = (
-                    acc[slot(i, z), :] + ways[way(last % 2, i, z), :]
-                )
+            plane_out[pl.ds(4 * (8 * x + z) + q, 8, stride=128), :] = total[8 * z : 8 * z + 8]
+
+    residuals(way_a, last_done)
 
     @pl.loop(1, NZ)
     def _(d):
@@ -414,8 +442,8 @@
         rows_of(plane_out, place * 4, 4, 4), rows_of(modes_in, mine * 4, 4, 4), self_sem.at[3]
     )
     keep_modes.start()
+    await_rows(modes_in, 1020, recv_sem.at[2])
     keep_modes.wait()
-    await_rows(modes_in, 1020, recv_sem.at[2])
     scattered(points_out, transform(table_ref[2], table_ref[3], gathered(modes_in)))
 
     @pl.loop(1, SPAN)
@@ -449,14 +477,20 @@
 
 def on_device(pressure_source, geometry, owner, eigen, steps, tables):
     vmem = pl.BlockSpec(memory_space=pltpu.VMEM)
+    hbm = pl.BlockSpec(memory_space=pltpu.HBM)
     smem = pl.BlockSpec(memory_space=pltpu.SMEM)
     cells = pltpu.VMEM((CELL_ROWS, LANES), F32)
     return pl.pallas_call(
         kernel,
         out_shape=jax.ShapeDtypeStruct(pressure_source.shape, F32),
-        in_specs=[vmem, vmem, smem, smem, smem, vmem],
+        in_specs=[hbm, hbm, smem, smem, smem, hbm],
         out_specs=vmem,
-        scratch_shapes=[cells] * 8
+        scratch_shapes=[
+            pltpu.VMEM(pressure_source.shape, F32),
+            pltpu.VMEM(geometry.shape[1:], F32),
+            pltpu.VMEM(tables.shape, BF16),
+        ]
+        + [cells] * 8
         + [
             pltpu.VMEM((784, LANES), F32),
             pltpu.VMEM((768, LANES), F32),
@@ -468,7 +502,9 @@
             pltpu.VMEM((4, CELL_ROWS, LANES), F32),
             cells,
             cells,
-            pltpu.VMEM((2304, LANES), F32),
+            cells,
+            cells,
+            pltpu.SemaphoreType.DMA((3,)),
             pltpu.SemaphoreType.DMA((4,)),
             pltpu.SemaphoreType.DMA((4,)),
             pltpu.SemaphoreType.DMA((7,)),

time: 129 us -> 103 us (0.80)
  Pallas kernels: 123 us -> 96.6 us
    pallas_call x1, Pallas kernels: 123 us -> 96.6 us  [on_device(): pl.pallas_call(kernel, out_shape=jax.ShapeDtypeStruct(pressure_source.sha...]
where the time goes in v2:
time: 103 us; the launch traced here: 102 us
  Pallas kernels  96.6 us (94%)
  local copies, waits for them, and re-layouts  4.54 us (4%)
    pallas_call x1, Pallas kernels, on_device(): pl.pallas_call(kernel, out_shape=jax.ShapeDtypeStruct(pressure_source.sha...  96.6 us
    unnamed x11, local copies, waits for them, and re-layouts  4.54 us

profile of v2, /device:TPU:6, one launch (start us, length us, event | category | flops | bytes accessed | tf_op | source)
XLA Modules:
  0.0 101.9 jit_solution(17367768968749012335)
XLA Ops:
  0.0 0.0 copy-start.4
  0.7 0.0 copy-start.3
  0.7 0.0 copy-done.4
  0.7 0.7 copy-done.3
  1.4 0.0 copy-start
  1.4 1.0 %copy-done = f32[4,32,1024]{2,1,0:T(8,128)S(1)} copy-done((f32[4,32,1024]{2,1,0:T(8,128)S(1)}, f32[4,32,1024]{2,1,0:T(8,128)}, u32[]{:S(2)}) %copy-start) | copy-done | bytes 524312
  2.4 0.0 copy-start.1
  2.4 1.0 %copy-done.1 = bf16[4,256,256]{2,1,0:T(8,128)(2,1)S(1)} copy-done((bf16[4,256,256]{2,1,0:T(8,128)(2,1)S(1)}, bf16[4,256,256]{2,1,0:T(8,128)(2,1)}, u32[]{:S(2)}) %copy-start.1) | copy-done | bytes 524312
  3.4 0.0 copy-start.2
  3.4 1.0 copy-done.2
  4.4 96.6 %shard_map.64 = f32[4,32,1024]{2,1,0:T(8,128)S(1)} custom-call(f32[4,32,1024]{2,1,0:T(8,128)S(1)} %copy-done, f32[3,32,1024]{2,1,0:T(8,128)S(1)} %bitcast.1, s32[1]{0:T(128)S(6)} %copy.8.owner_ref, f32[256]{0:T(256)S(1)} %copy-done.4, f32[2,16]{1,0:T(2,128)S(1)} %copy-done.3, bf16[4,256,256]{2,1,0:T(8,128)(2,1)S(1)} %copy-done.1), custom_call_target="tpu_custom_call" | custom-call | tf_op jit(solution)/shard_map/pallas_call | solution.py:483
  101.1 0.8 copy.9
Async XLA Ops:
  0.0 0.7 copy-start.4
  0.7 0.7 copy-start.3
  1.4 1.0 %copy-start = (f32[4,32,1024]{2,1,0:T(8,128)S(1)}, f32[4,32,1024]{2,1,0:T(8,128)}, u32[]{:S(2)}) copy-start(f32[4,32,1024]{2,1,0:T(8,128)} %x_hbm.1) | copy-start | bytes 1572868
  2.4 1.0 %copy-start.1 = (bf16[4,256,256]{2,1,0:T(8,128)(2,1)S(1)}, bf16[4,256,256]{2,1,0:T(8,128)(2,1)}, u32[]{:S(2)}) copy-start(bf16[4,256,256]{2,1,0:T(8,128)(2,1)} %constant.8.clone.table_hbm) | copy-start | bytes 1572868
  3.4 1.0 copy-start.2

commit v3 on v2

--- a/solution.py
+++ b/solution.py
@@ -106,8 +106,6 @@
     masked,
     part_x,
     sum_x,
-    part_y,
-    sum_y,
     part_z,
     geo,
     coef,
@@ -132,12 +130,20 @@
     mine = span * 4 + row
     place = 64 * row + span
 
+    def far_first(k, n):
+        step = lax.div(k + 1, 2)
+        return lax.rem(n // 2 + step + lax.rem(k, 2) * (n - 2 * step), n)
+
     def span_peer(d):
-        dz, dx, dy = lax.rem(d, 8), lax.rem(lax.div(d, 8), 4), lax.div(d, 32)
-        return lax.rem(yh + dy, 2) * 32 + lax.rem(xi + dx, 4) * 8 + lax.rem(zi + dz, 8)
+        zk, xk, yk = lax.rem(d, 8), lax.rem(lax.div(d, 8), 4), lax.div(d, 32)
+        return (
+            lax.rem(yh + 1 - yk, 2) * 32
+            + lax.rem(xi + far_first(xk, 4), 4) * 8
+            + lax.rem(zi + far_first(zk, 8), 8)
+        )
 
     def any_peer(d):
-        dc, dl = lax.rem(d, 2), lax.rem(lax.div(d, 2), 2)
+        dc, dl = 1 - lax.rem(d, 2), 1 - lax.rem(lax.div(d, 2), 2)
         return span_peer(lax.div(d, 4)), lax.rem(yl + dl, 2) * 2 + lax.rem(core + dc, 2)
 
     def rows_of(ref, start, size, unit):
@@ -167,7 +173,7 @@
 
     barrier = pltpu.get_barrier_semaphore()
 
-    @pl.loop(1, SPAN)
+    @pl.loop(0, SPAN - 1)
     def _(d):
         pl.semaphore_signal(barrier, inc=1, device_id=(span_peer(d), row), device_id_type=MESH)
 
@@ -216,7 +222,7 @@
     def sems(k):
         return send_sem.at[k], recv_sem.at[k]
 
-    @pl.loop(1, SPAN)
+    @pl.loop(0, SPAN - 1)
     def _(d):
         to = span_peer(d)
         push(
@@ -235,50 +241,62 @@
 
     await_rows(part_x, 576, geo_recv.at[0])
     sum_x[...] = part_x[0:192] + part_x[192:384] + part_x[384:576] + part_x[576:768]
-    push(
-        rows_of(sum_x, (1 - yh) * 96, 96, 8),
-        part_y,
-        geo_sems(1),
-        (span_at(1 - yh, xi, zi), row),
-    )
-    await_rows(part_y, 96, geo_recv.at[1])
-    sum_y[...] = part_y[...] + sum_x[pl.ds(pl.multiple_of(yh * 96, 8), 96), :]
-    for d in range(1, 8):
-        to = lax.rem(zi + d, 8)
-        push(
-            rows_of(sum_y, to * 12, 12, 4),
-            rows_of(part_z, zi * 16, 12, 4),
-            geo_sems(2),
-            (span_at(yh, xi, to), row),
+    others = [(dy, dz) for dz in (4, 3, 5, 2, 6, 1, 7, 0) for dy in (1, 0)][:-1]
+    others = [(lax.rem(yh + dy, 2), lax.rem(zi + dz, 8)) for dy, dz in others]
+    part_here = 16 * (8 * yh + zi)
+    for y_to, z_to in others:
+        push(
+            rows_of(sum_x, 12 * (8 * y_to + z_to), 12, 4),
+            rows_of(part_z, part_here, 12, 4),
+            geo_sems(1),
+            (span_at(y_to, xi, z_to), row),
         )
     keep_z = pltpu.make_async_copy(
-        rows_of(sum_y, zi * 12, 12, 4), rows_of(part_z, zi * 16, 12, 4), self_sem.at[0]
+        rows_of(sum_x, 12 * (8 * yh + zi), 12, 4),
+        rows_of(part_z, part_here, 12, 4),
+        self_sem.at[0],
     )
     keep_z.start()
-    await_rows(part_z, 84, geo_recv.at[2])
+    await_rows(part_z, 180, geo_recv.at[1])
     keep_z.wait()
     total = part_z[0:12]
-    for d in range(1, 8):
+    for d in range(1, 16):
         total = total + part_z[16 * d : 16 * d + 12]
-    sum_y_own = masked.at[pl.ds(768, 12)]
+    sum_own = masked.at[pl.ds(768, 12)]
     masked[768:780, :] = total
 
     here = 12 * place
-    for d in range(1, 8):
-        push(
-            sum_y_own,
+    for y_to, z_to in others:
+        push(
+            sum_own,
             rows_of(geo, here, 12, 4),
-            geo_sems(3),
-            (span_at(yh, xi, lax.rem(zi + d, 8)), row),
-        )
-    keep_geo = pltpu.make_async_copy(sum_y_own, rows_of(geo, here, 12, 4), self_sem.at[1])
+            geo_sems(2),
+            (span_at(y_to, xi, z_to), row),
+        )
+    keep_geo = pltpu.make_async_copy(sum_own, rows_of(geo, here, 12, 4), self_sem.at[1])
     keep_geo.start()
 
     await_rows(cells_in, 1008, recv_sem.at[0])
     fetch[2].wait()
     scattered(modes_out, transform(table_ref[0], table_ref[1], gathered(cells_in)))
 
-    @pl.loop(1, NZ)
+    def block(r, y, x):
+        return rows_of(geo, 12 * (64 * r + 32 * y + 8 * x), 96, 8)
+
+    await_rows(geo, 180, geo_recv.at[2])
+    keep_geo.wait()
+    for dx, dl in ((2, 1), (1, 1), (3, 1), (2, 0), (1, 0), (3, 0), (0, 1)):
+        x_to, l_to = lax.rem(xi + dx, 4), lax.rem(yl + dl, 2)
+        for y in range(2):
+            push(
+                block(row, y, xi),
+                block(row, y, xi),
+                (geo_send.at[3], geo_recv.at[4 + dx]),
+                (span_at(yh, x_to, zi), 2 * l_to + core),
+            )
+
+
+    @pl.loop(0, NZ - 1)
     def _(d):
         to_span, to_row = any_peer(d)
         push(
@@ -293,39 +311,18 @@
     )
     keep_plane.start()
 
-    def block(r, y, x):
-        return rows_of(geo, 12 * (64 * r + 32 * y + 8 * x), 96, 8)
-
-    await_rows(geo, 84, geo_recv.at[3])
-    keep_geo.wait()
-    for d in range(1, 4):
-        y_to, l_to = lax.rem(yh + d // 2, 2), lax.rem(yl + d % 2, 2)
-        push(
-            block(row, yh, xi),
-            block(row, yh, xi),
-            geo_sems(4),
-            (span_at(y_to, xi, zi), 2 * l_to + core),
-        )
-    await_rows(geo, 288, geo_recv.at[4])
-    for d in range(1, 4):
-        to = lax.rem(xi + d, 4)
+    for dx, count in ((0, 192), (1, 384), (3, 384), (2, 384)):
+        await_rows(geo, count, geo_recv.at[4 + dx])
         for l in range(2):
             for y in range(2):
+                whole_block = block(2 * l + core, y, lax.rem(xi + 4 - dx, 4))
                 push(
-                    block(2 * l + core, y, xi),
-                    block(2 * l + core, y, xi),
-                    geo_sems(5),
-                    (span_at(yh, to, zi), row),
+                    whole_block,
+                    whole_block,
+                    (geo_send.at[4], geo_recv.at[3]),
+                    (span, 2 * yl + 1 - core),
                 )
-    await_rows(geo, 1152, geo_recv.at[5])
-    for l in range(2):
-        push(
-            rows_of(geo, 768 * (2 * l + core), 768, 8),
-            rows_of(geo, 768 * (2 * l + core), 768, 8),
-            geo_sems(6),
-            (span, 2 * yl + 1 - core),
-        )
-    await_rows(geo, 1536, geo_recv.at[6])
+    await_rows(geo, 1536, geo_recv.at[3])
 
     await_rows(plane_in, 1020, recv_sem.at[1])
     keep_plane.wait()
@@ -428,7 +425,7 @@
 
     residuals(way_a, last_done)
 
-    @pl.loop(1, NZ)
+    @pl.loop(0, NZ - 1)
     def _(d):
         to_span, to_row = any_peer(d)
         push(
@@ -446,7 +443,7 @@
     keep_modes.wait()
     scattered(points_out, transform(table_ref[2], table_ref[3], gathered(modes_in)))
 
-    @pl.loop(1, SPAN)
+    @pl.loop(0, SPAN - 1)
     def _(d):
         to = span_peer(d)
         push(
@@ -471,7 +468,7 @@
     await_rows(modes_out, 1020, send_sem.at[1])
     await_rows(plane_out, 1020, send_sem.at[2])
     await_rows(points_out, 1008, send_sem.at[3])
-    for k, count in enumerate((576, 96, 84, 84, 288, 1152, 1536)):
+    for k, count in enumerate((576, 180, 180, 1344, 1536)):
         await_rows(geo, count, geo_send.at[k])
 
 
@@ -495,9 +492,7 @@
             pltpu.VMEM((784, LANES), F32),
             pltpu.VMEM((768, LANES), F32),
             pltpu.VMEM((192, LANES), F32),
-            pltpu.VMEM((96, LANES), F32),
-            pltpu.VMEM((96, LANES), F32),
-            pltpu.VMEM((128, LANES), F32),
+            pltpu.VMEM((256, LANES), F32),
             pltpu.VMEM((3072, LANES), F32),
             pltpu.VMEM((4, CELL_ROWS, LANES), F32),
             cells,
@@ -507,8 +502,8 @@
             pltpu.SemaphoreType.DMA((3,)),
             pltpu.SemaphoreType.DMA((4,)),
             pltpu.SemaphoreType.DMA((4,)),
-            pltpu.SemaphoreType.DMA((7,)),
-            pltpu.SemaphoreType.DMA((7,)),
+            pltpu.SemaphoreType.DMA((5,)),
+            pltpu.SemaphoreType.DMA((8,)),
             pltpu.SemaphoreType.DMA((4,)),
         ],
         compiler_params=pltpu.CompilerParams(

time: 103 us -> 93.6 us (0.909)
  Pallas kernels: 96.6 us -> 87.4 us
    pallas_call x1, Pallas kernels: 96.6 us -> 87.4 us  [on_device(): pl.pallas_call(kernel, out_shape=jax.ShapeDtypeStruct(pressure_source.sha...]
where the time goes in v3:
time: 93.6 us; the launch traced here: 92.7 us
  Pallas kernels  87.4 us (93%)
  local copies, waits for them, and re-layouts  4.54 us (5%)
    pallas_call x1, Pallas kernels, on_device(): pl.pallas_call(kernel, out_shape=jax.ShapeDtypeStruct(pressure_source.sha...  87.4 us
    unnamed x11, local copies, waits for them, and re-layouts  4.54 us

profile of v3, /device:TPU:6, one launch (start us, length us, event | category | flops | bytes accessed | tf_op | source)
XLA Modules:
  0.0 92.7 jit_solution(12709016587312412603)
XLA Ops:
  0.0 0.0 copy-start.4
  0.7 0.0 copy-start.3
  0.7 0.0 copy-done.4
  0.7 0.7 copy-done.3
  1.4 0.0 copy-start
  1.4 1.0 %copy-done = f32[4,32,1024]{2,1,0:T(8,128)S(1)} copy-done((f32[4,32,1024]{2,1,0:T(8,128)S(1)}, f32[4,32,1024]{2,1,0:T(8,128)}, u32[]{:S(2)}) %copy-start) | copy-done | bytes 524312
  2.4 0.0 copy-start.1
  2.4 1.0 %copy-done.1 = bf16[4,256,256]{2,1,0:T(8,128)(2,1)S(1)} copy-done((bf16[4,256,256]{2,1,0:T(8,128)(2,1)S(1)}, bf16[4,256,256]{2,1,0:T(8,128)(2,1)}, u32[]{:S(2)}) %copy-start.1) | copy-done | bytes 524312
  3.4 0.0 copy-start.2
  3.4 1.0 %copy-done.2 = f32[1,3,32,1024]{3,2,1,0:T(8,128)S(1)} copy-done((f32[1,3,32,1024]{3,2,1,0:T(8,128)S(1)}, f32[1,3,32,1024]{3,2,1,0:T(8,128)}, u32[]{:S(2)}) %copy-start.2) | copy-done | bytes 393240
  4.4 87.4 %shard_map.64 = f32[4,32,1024]{2,1,0:T(8,128)S(1)} custom-call(f32[4,32,1024]{2,1,0:T(8,128)S(1)} %copy-done, f32[3,32,1024]{2,1,0:T(8,128)S(1)} %bitcast.1, s32[1]{0:T(128)S(6)} %copy.8.owner_ref, f32[256]{0:T(256)S(1)} %copy-done.4, f32[2,16]{1,0:T(2,128)S(1)} %copy-done.3, bf16[4,256,256]{2,1,0:T(8,128)(2,1)S(1)} %copy-done.1), custom_call_target="tpu_custom_call" | custom-call | tf_op jit(solution)/shard_map/pallas_call | solution.py:480
  91.9 0.8 copy.9
Async XLA Ops:
  0.0 0.7 copy-start.4
  0.7 0.7 copy-start.3
  1.4 1.0 %copy-start = (f32[4,32,1024]{2,1,0:T(8,128)S(1)}, f32[4,32,1024]{2,1,0:T(8,128)}, u32[]{:S(2)}) copy-start(f32[4,32,1024]{2,1,0:T(8,128)} %x_hbm.1) | copy-start | bytes 1572868
  2.4 1.0 %copy-start.1 = (bf16[4,256,256]{2,1,0:T(8,128)(2,1)S(1)}, bf16[4,256,256]{2,1,0:T(8,128)(2,1)}, u32[]{:S(2)}) copy-start(bf16[4,256,256]{2,1,0:T(8,128)(2,1)} %constant.8.clone.table_hbm) | copy-start | bytes 1572868
  3.4 1.0 %copy-start.2 = (f32[1,3,32,1024]{3,2,1,0:T(8,128)S(1)}, f32[1,3,32,1024]{3,2,1,0:T(8,128)}, u32[]{:S(2)}) copy-start(f32[1,3,32,1024]{3,2,1,0:T(8,128)} %param.7) | copy-start | bytes 1179652

commit v4 on v3

--- a/solution.py
+++ b/solution.py
@@ -324,8 +324,6 @@
                 )
     await_rows(geo, 1536, geo_recv.at[3])
 
-    await_rows(plane_in, 1020, recv_sem.at[1])
-    keep_plane.wait()
 
     eigen = eigen_ref[mine]
     lane = lax.broadcasted_iota(jnp.int32, (8, LANES), 1)
@@ -364,7 +362,16 @@
                 coef[1, slot(i, z), :] = east * inverse
                 coef[2, slot(i, z), :] = north_in * inverse
                 coef[3, slot(i, z), :] = south * inverse
-                value = plane_in[pl.ds(4 * (8 * x + z) + q, 8, stride=128), :] * inverse
+                way_b[slot(i, z), :] = inverse
+
+    await_rows(plane_in, 1020, recv_sem.at[1])
+    keep_plane.wait()
+    for x in range(4):
+        for q in range(4):
+            i = 4 * x + q
+            for z in range(8):
+                value = plane_in[pl.ds(4 * (8 * x + z) + q, 8, stride=128), :]
+                value = value * way_b[slot(i, z), :]
                 zed[slot(i, z), :] = value
                 way_a[slot(i, z), :] = value * (1.0 / CENTER)
                 acc[slot(i, z), :] = jnp.zeros((8, LANES), F32)

time: 93.6 us -> 92.6 us (0.989)
  Pallas kernels: 87.4 us -> 86.3 us
    pallas_call x1, Pallas kernels: 87.4 us -> 86.3 us  [on_device(): pl.pallas_call(kernel, out_shape=jax.ShapeDtypeStruct(pressure_source.sha...]
where the time goes in v4:
time: 92.6 us; the launch traced here: 91.6 us
  Pallas kernels  86.3 us (93%)
  local copies, waits for them, and re-layouts  4.54 us (5%)
    pallas_call x1, Pallas kernels, on_device(): pl.pallas_call(kernel, out_shape=jax.ShapeDtypeStruct(pressure_source.sha...  86.3 us
    unnamed x11, local copies, waits for them, and re-layouts  4.54 us

profile of v4, /device:TPU:6, one launch (start us, length us, event | category | flops | bytes accessed | tf_op | source)
XLA Modules:
  0.0 91.6 jit_solution(3965988715967176882)
XLA Ops:
  0.0 0.0 copy-start.4
  0.7 0.0 copy-start.3
  0.7 0.0 copy-done.4
  0.7 0.7 copy-done.3
  1.4 0.0 copy-start
  1.4 1.0 %copy-done = f32[4,32,1024]{2,1,0:T(8,128)S(1)} copy-done((f32[4,32,1024]{2,1,0:T(8,128)S(1)}, f32[4,32,1024]{2,1,0:T(8,128)}, u32[]{:S(2)}) %copy-start) | copy-done | bytes 524312
  2.4 0.0 copy-start.1
  2.4 1.0 %copy-done.1 = bf16[4,256,256]{2,1,0:T(8,128)(2,1)S(1)} copy-done((bf16[4,256,256]{2,1,0:T(8,128)(2,1)S(1)}, bf16[4,256,256]{2,1,0:T(8,128)(2,1)}, u32[]{:S(2)}) %copy-start.1) | copy-done | bytes 524312
  3.4 0.0 copy-start.2
  3.4 1.0 %copy-done.2 = f32[1,3,32,1024]{3,2,1,0:T(8,128)S(1)} copy-done((f32[1,3,32,1024]{3,2,1,0:T(8,128)S(1)}, f32[1,3,32,1024]{3,2,1,0:T(8,128)}, u32[]{:S(2)}) %copy-start.2) | copy-done | bytes 393240
  4.4 86.3 %shard_map.64 = f32[4,32,1024]{2,1,0:T(8,128)S(1)} custom-call(f32[4,32,1024]{2,1,0:T(8,128)S(1)} %copy-done, f32[3,32,1024]{2,1,0:T(8,128)S(1)} %bitcast.1, s32[1]{0:T(128)S(6)} %copy.8.owner_ref, f32[256]{0:T(256)S(1)} %copy-done.4, f32[2,16]{1,0:T(2,128)S(1)} %copy-done.3, bf16[4,256,256]{2,1,0:T(8,128)(2,1)S(1)} %copy-done.1), custom_call_target="tpu_custom_call" | custom-call | tf_op jit(solution)/shard_map/pallas_call | solution.py:487
  90.8 0.8 copy.9
Async XLA Ops:
  0.0 0.7 copy-start.4
  0.7 0.7 copy-start.3
  1.4 1.0 %copy-start = (f32[4,32,1024]{2,1,0:T(8,128)S(1)}, f32[4,32,1024]{2,1,0:T(8,128)}, u32[]{:S(2)}) copy-start(f32[4,32,1024]{2,1,0:T(8,128)} %x_hbm.1) | copy-start | bytes 1572868
  2.4 1.0 %copy-start.1 = (bf16[4,256,256]{2,1,0:T(8,128)(2,1)S(1)}, bf16[4,256,256]{2,1,0:T(8,128)(2,1)}, u32[]{:S(2)}) copy-start(bf16[4,256,256]{2,1,0:T(8,128)(2,1)} %constant.8.clone.table_hbm) | copy-start | bytes 1572868
  3.4 1.0 %copy-start.2 = (f32[1,3,32,1024]{3,2,1,0:T(8,128)S(1)}, f32[1,3,32,1024]{3,2,1,0:T(8,128)}, u32[]{:S(2)}) copy-start(f32[1,3,32,1024]{3,2,1,0:T(8,128)} %param.7) | copy-start | bytes 1179652
